TPU v7x, 256 devices: a whole 4x4x8 slice. The times are simulated.
256 devices in a mesh: gx: 32 (over y_hi, z, core), az: 8 (over y_lo, x).
Axes of the slice: x: 4, y: 4 (y_hi: 2, y_lo: 2; y = y_hi * 2 + y_lo), z: 8, core: 2. Of those that a mesh axis runs over, the one named last changes fastest.
Arguments:
- state: float32 [5, 512, 256, 512], P(None, 'gx', 'az'), as said below
- sponge_level: int32 [512, 256, 512], P('gx', 'az'), may hold values from 0 to 3
- inv_dx: float32 [512], P('gx'), may hold values from 1 to 8
- inv_dr: float32 [512], replicated, may hold values from 1 to 8
- target: float32 [5, 512], replicated, may hold values from -4 to 4
- cutoff: int32 [32], replicated, may hold values from 2 to 32, as said below
Outputs:
- section_state: float32 [5, 512, 256, 512], P(None, 'gx', 'az')
Inputs may be any that keep to these rules, and one draw needn't show every extreme that they name: `cutoff`: every value from 2 to 32 may occur; both ends occur on some cycle. `state`: density lies between 0.7 and 1.3 and pressure is positive.
All inputs are finite; a program needn't handle non-finite values.
Results may differ from a plain program's by a relative error of at most 0.0003.
Values sent between devices are 32-bit elements; how exact they have to be, the bound alone decides.
A program may use at most 128 MiB of HBM per device.

v0:
```python
import jax
import jax.numpy as jnp
from jax import lax
from jax.sharding import PartitionSpec as P

NT = 256
CYCLE = 32


gas_factor = 0.4
time_step = 0.02
sponge_rate = 4.0


def extended(cells, sides, width, closed):
    for axis, dim in sides:
        count = lax.axis_size(axis)
        ends = count if closed else count - 1
        head = lax.slice_in_dim(cells, 0, width, axis=dim)
        tail = lax.slice_in_dim(cells, cells.shape[dim] - width, cells.shape[dim], axis=dim)
        cells = jnp.concatenate(
            [
                lax.ppermute(tail, axis, [(i, (i + 1) % count) for i in range(ends)]),
                cells,
                lax.ppermute(head, axis, [((i + 1) % count, i) for i in range(ends)]),
            ],
            axis=dim,
        )
    return cells


def cycle_radius(length):
    return 1.0 + 4.0 * jnp.arange(length, dtype=jnp.float32) / length


def flux_parts(fields, radius):
    density = fields[0]
    axial_momentum = fields[1]
    radial_momentum = fields[2]
    swirl_momentum = fields[3]
    energy = fields[4]
    axial_speed = axial_momentum / density
    radial_speed = radial_momentum / density
    swirl_speed = swirl_momentum / density
    pressure = gas_factor * (
        energy
        - 0.5
        * (
            axial_momentum * axial_speed
            + radial_momentum * radial_speed
            + swirl_momentum * swirl_speed
        )
    )
    enthalpy = energy + pressure
    axial_flux = jnp.stack(
        [
            axial_momentum,
            axial_momentum * axial_speed + pressure,
            radial_momentum * axial_speed,
            swirl_momentum * axial_speed,
            enthalpy * axial_speed,
        ]
    )
    radial_flux = radius * jnp.stack(
        [
            radial_momentum,
            axial_momentum * radial_speed,
            radial_momentum * radial_speed + pressure,
            swirl_momentum * radial_speed,
            enthalpy * radial_speed,
        ]
    )
    swirl_flux = jnp.stack(
        [
            swirl_momentum,
            axial_momentum * swirl_speed,
            radial_momentum * swirl_speed,
            swirl_momentum * swirl_speed + pressure,
            enthalpy * swirl_speed,
        ]
    )
    press_source = (pressure + swirl_momentum * swirl_speed) / radius
    turn_source = -(radial_momentum * swirl_speed) / radius
    return (axial_flux, radial_flux, swirl_flux, press_source, turn_source)


def mode_tables(mode_count, length):
    wave_number = (
        jnp.arange(mode_count, dtype=jnp.int32)[:, None]
        * jnp.arange(length, dtype=jnp.int32)[None, :]
    )
    phase_angle = 2.0 * jnp.pi / length * (wave_number % length).astype(jnp.float32)
    return (jnp.cos(phase_angle), jnp.sin(phase_angle))


def mode_weights(mode_count, length, cycle_cut):
    wave_number = jnp.arange(mode_count, dtype=jnp.int32)[:, None]
    mode_scale = jnp.where(wave_number == 0, 1.0, 2.0) / length
    return jnp.where(wave_number <= cycle_cut[None, :], mode_scale, 0.0).astype(jnp.float32)


def forward(values_block, cosine, sine):
    forward_cos = jnp.einsum("itr,kt->ikr", values_block, cosine, precision=lax.Precision.HIGHEST)
    forward_sin = jnp.einsum("itr,kt->ikr", values_block, sine, precision=lax.Precision.HIGHEST)
    return (forward_cos, forward_sin)


def inverse(coef_cos, coef_sin, weights, cosine, sine):
    first_part = jnp.einsum(
        "ikr,kt->itr", coef_cos * weights[None], cosine, precision=lax.Precision.HIGHEST
    )
    second_part = jnp.einsum(
        "ikr,kt->itr", coef_sin * weights[None], sine, precision=lax.Precision.HIGHEST
    )
    return first_part + second_part


def body(state, sponge_level, inv_dx, inv_dr, target, cutoff):
    planes = state.shape[1]
    columns = state.shape[2]
    cycles_all = state.shape[3]
    radius = cycle_radius(cycles_all)
    axial_flux, radial_flux, swirl_flux, press_source, turn_source = flux_parts(state, radius)
    axial_wide = extended(axial_flux, (("gx", 1),), 1, False)
    swirl_wide = extended(swirl_flux, (("az", 2),), 1, True)
    axial_term = (axial_wide[:, 2:] - axial_wide[:, :-2]) * (0.5 * inv_dx)[None, :, None, None]
    radial_pad = jnp.pad(radial_flux, ((0, 0), (0, 0), (0, 0), (1, 1)))
    radial_term = (radial_pad[..., 2:] - radial_pad[..., :-2]) * (0.5 * inv_dr / radius)
    swirl_term = (swirl_wide[:, :, 2:] - swirl_wide[:, :, :-2]) * (NT / (4.0 * jnp.pi) / radius)
    tendency = -(axial_term + radial_term + swirl_term)
    zero_field = jnp.zeros_like(press_source)
    tendency = tendency + jnp.stack([zero_field, zero_field, press_source, turn_source, zero_field])
    tendency = tendency - sponge_rate * sponge_level.astype(jnp.float32)[None] * (
        state - target[:, None, None, :]
    )
    updated = state + time_step * tendency
    inner_block = updated[..., :CYCLE].reshape(5 * planes, columns, CYCLE)
    mode_count = NT // 8 + 1
    cosine, sine = mode_tables(mode_count, NT)
    position = lax.axis_index("az")
    cycle_share = CYCLE // lax.axis_size("az")
    cycle_cut = lax.dynamic_slice_in_dim(cutoff, position * cycle_share, cycle_share, 0)
    weights = mode_weights(mode_count, NT, cycle_cut)
    coef_cos, coef_sin = forward(
        lax.all_to_all(inner_block, "az", split_axis=2, concat_axis=1, tiled=True), cosine, sine
    )
    turned = inverse(coef_cos, coef_sin, weights, cosine, sine)
    filtered = lax.all_to_all(turned, "az", split_axis=1, concat_axis=2, tiled=True)
    filtered = filtered.reshape(5, planes, columns, CYCLE)
    return jnp.concatenate([filtered, updated[..., CYCLE:]], axis=3)


def solution(mesh):
    return jax.shard_map(
        body,
        mesh=mesh,
        in_specs=(P(None, "gx", "az", None), P("gx", "az", None), P("gx"), P(), P(), P()),
        out_specs=P(None, "gx", "az", None),
        check_vma=False,
    )
```

profile of v0, /device:TPU:1, one launch (start us, length us, event | category | flops | bytes accessed | tf_op | source)
XLA Modules:
  0.0 90.3 jit_solution(13075057641744212427)
XLA Ops:
  0.0 3.5 %broadcast_divide_fusion = (f32[1,16,32,512]{3,2,1,0:T(8,128)S(1)}, f32[1,16,32,512]{3,2,1,0:T(8,128)S(1)}, f32[1,16,32,512]{3,2,1,0:T(8,128)S(1)}, f32[1,16,32,...) fusion(f32[512]{0:T(512)S(1)} %multiply_add_fusion, f32[5,16,32,512]{3,2,1,0:T(8,128)} %param.6), kind=kLoop, calls=%fused_computation.51 | loop fusion | flops 3407871 | bytes 11536384 | tf_op jit(solution)/shard_map/div | solution.py:82
  3.5 0.6 copy-done
  4.1 0.3 slice_dynamic-update-slice_fusion.2
  4.4 0.2 fusion.16
  4.7 0.8 add_dynamic-update-slice_fusion.1
  5.5 0.3 multiply_dynamic-update-slice_fusion.7
  5.8 0.6 multiply_dynamic-update-slice_fusion.6
  6.4 1.1 %negate_divide_fusion = (f32[1,16,32,512]{3,2,1,0:T(8,128)S(1)}, f32[5,16,32,512]{3,2,1,0:T(8,128)S(1)}, f32[5,16,32,512]{3,2,1,0:T(8,128)S(1)}, f32[5,16,32,512]{3,2,1,0:T(8,128)S(1)}) fusion(f32[512]{0:T(512)S(1)} %multiply_add_fusion, f32[1,16,32,512]{3,2,1,0:T(8,128)S(1)} %get-tuple-element.7, f32[5,16,32,512]{3,2,1,0:T(8,128)S(1)} %copy-done, ...), kind=kLoop, calls=%fused_computation.28 | loop fusion | flops 2097152 | bytes 10487808 | tf_op jit(solution)/shard_map/div | solution.py:83
  7.5 1.0 %fusion.53 = (f32[5,1,32,512]{3,2,1,0:T(8,128)}, f32[5,1,32,512]{3,2,1,0:T(8,128)}) fusion(f32[5,16,32,512]{3,2,1,0:T(8,128)S(1)} %get-tuple-element.12), kind=kLoop, calls=%fused_computation.94 | loop fusion | bytes 1310720 | tf_op jit(solution)/shard_map/slice | solution.py:19
  8.5 5.1 %collective-permute-start = (f32[5,1,32,512]{3,2,1,0:T(8,128)}, f32[5,1,32,512]{3,2,1,0:T(8,128)S(1)}, u32[]{:S(2)}, u32[]{:S(2)}) collective-permute-start(f32[5,1,32,512]{3,2,1,0:T(8,128)} %get-tuple-element.16), channel_id=1, source_target_pairs={{8,0},{16,8},{24,16},{32,24},{40,32},{48,40},{56,48},{64,56},{72,6... | collective-permute-start | bytes 983048 | tf_op jit(solution)/shard_map/ppermute | solution.py:25
  13.6 1.9 %collective-permute-start.1 = (f32[5,1,32,512]{3,2,1,0:T(8,128)}, f32[5,1,32,512]{3,2,1,0:T(8,128)}, u32[]{:S(2)}, u32[]{:S(2)}) collective-permute-start(f32[5,1,32,512]{3,2,1,0:T(8,128)} %get-tuple-element.17), channel_id=1, source_target_pairs={{0,8},{8,16},{16,24},{24,32},{32,40},{40,48},{48,56},{56,64},{64,7... | collective-permute-start | bytes 983048 | tf_op jit(solution)/shard_map/ppermute | solution.py:23
  15.5 0.3 fusion.54
  15.8 0.7 copy.38
  16.5 3.3 %collective-permute-start.2 = (f32[5,16,1,512]{3,1,2,0:T(8,128)}, f32[5,16,1,512]{3,1,2,0:T(8,128)}, u32[]{:S(2)}, u32[]{:S(2)}) collective-permute-start(f32[5,16,1,512]{3,1,2,0:T(8,128)} %copy.38), channel_id=1, source_target_pairs={{1,0},{2,1},{3,2},{4,3},{5,4},{6,5},{7,6},{0,7},{9,8},{10,9},{11,1... | collective-permute-start | bytes 491528 | tf_op jit(solution)/shard_map/ppermute | solution.py:25
  19.8 0.7 copy.40
  20.5 0.0 collective-permute-start.3
  20.5 0.2 multiply_dynamic-update-slice_fusion.3
  20.7 0.4 multiply_dynamic-update-slice_fusion.2
  21.1 0.0 copy-start.3
  21.2 0.0 copy-start.5
  21.2 0.0 copy-start.6
  21.2 0.0 copy-start.7
  21.2 0.0 copy-start.4
  21.2 3.0 %broadcast_multiply_fusion = f32[5,16,32,512]{3,2,1,0:T(8,128)} fusion(f32[5,16,32,512]{3,2,1,0:T(8,128)S(1)} %multiply_dynamic-update-slice_fusion.2, f32[512]{0:T(512)S(1)} %multiply_add_fusion), kind=kLoop, calls=%fused_computation.20 | loop fusion | flops 1310720 | bytes 10487808 | tf_op jit(solution)/shard_map/mul | solution.py:64
  24.2 0.1 convert_multiply_fusion
  24.4 0.1 pad.10.clone
  24.5 0.1 dynamic_slice.3
  24.6 0.0 collective-permute-done.2
  24.6 1.1 %copy.39 = f32[5,16,1,512]{3,2,1,0:T(1,128)S(1)} copy(f32[5,16,1,512]{3,1,2,0:T(8,128)} %collective-permute-done.2) | data formatting | bytes 327680 | tf_op jit(solution)/shard_map/ppermute | solution.py:25
  25.7 4.8 %collective-permute-done.3 = f32[5,16,1,512]{3,1,2,0:T(8,128)} collective-permute-done((f32[5,16,1,512]{3,1,2,0:T(8,128)}, f32[5,16,1,512]{3,1,2,0:T(8,128)}, u32[]{:S(2)}, u32[]{:S(2)}) %collective-permute-start.3) | collective-permute-done | bytes 163872 | tf_op jit(solution)/shard_map/ppermute | solution.py:23
  30.5 1.1 %copy.41 = f32[5,16,1,512]{3,2,1,0:T(1,128)S(1)} copy(f32[5,16,1,512]{3,1,2,0:T(8,128)} %collective-permute-done.3) | data formatting | bytes 327680 | tf_op jit(solution)/shard_map/ppermute | solution.py:23
  31.6 17.8 %fusion.8 = f32[5,16,32,512]{3,2,1,0:T(8,128)} fusion(f32[5,16,32,512]{3,2,1,0:T(8,128)} %param.6, f32[5,16,32,512]{3,2,1,0:T(8,128)} %broadcast_multiply_fusion, f32[5,16,32,512]{3,2,1,0:T(8,128)} %copy-done.2, f32[5,16,1,512]{3,2,1,0:T(1,128)S(1)} %copy.41, f32[5,16,1,512]{3,2,1,0:T(1,128)S(1)} %copy.39, f32[5,16,32,512]{3,2,1,0:T(8,128)} %copy-done.1, ...), kind=kLoop, calls=%fused_computation.10 | loop fusion | flops 28835840 | bytes 30357608 | tf_op jit(solution)/shard_map/add | solution.py:136
  49.4 1.4 %slice.76 = f32[5,16,32,32]{3,2,1,0:T(8,128)S(1)} slice(f32[5,16,32,512]{3,2,1,0:T(8,128)} %fusion.8), slice={[0:5], [0:16], [0:32], [0:32]} | slice | bytes 655360 | tf_op jit(solution)/shard_map/slice | solution.py:137
  50.8 1.7 %copy.42 = f32[80,32,32]{0,1,2:T(8,128)} copy(f32[80,32,32]{2,1,0:T(8,128)S(1)} %bitcast.31) | data formatting | bytes 655360 | tf_op jit(solution)/shard_map/reshape | solution.py:137
  52.5 3.5 %all-to-all-start = ((f32[80,32,32]{0,1,2:T(8,128)}), f32[80,32,32]{0,1,2:T(8,128)S(1)}, u32[]{:S(2)}, u32[]{:S(2)}) async-start(f32[80,32,32]{0,1,2:T(8,128)} %copy.42), calls=%async_computation | async-start | bytes 1048576 | tf_op jit(solution)/shard_map/all_to_all | solution.py:145
  56.0 0.1 fusion.34
  56.1 9.8 %all-to-all-done = f32[80,32,32]{0,1,2:T(8,128)S(1)} async-done(((f32[80,32,32]{0,1,2:T(8,128)}), f32[80,32,32]{0,1,2:T(8,128)S(1)}, u32[]{:S(2)}, u32[]{:S(2)}) %all-to-all-start) | async-done | bytes 327712 | tf_op jit(solution)/shard_map/all_to_all | solution.py:145
  66.0 0.6 fusion.15
  66.6 0.6 fusion.14
  67.2 0.6 fusion.22
  67.8 0.6 fusion.13
  68.4 1.0 %copy.46 = f32[80,256,4]{0,2,1:T(4,128)} copy(f32[80,256,4]{1,0,2:T(8,128)S(1)} %fusion.13) | data formatting | bytes 655360 | tf_op jit(solution)/shard_map/add | solution.py:115
  69.4 3.7 %all-to-all-start.1 = ((f32[80,256,4]{0,2,1:T(4,128)}), f32[80,256,4]{0,2,1:T(4,128)S(1)}, u32[]{:S(2)}, u32[]{:S(2)}) async-start(f32[80,256,4]{0,2,1:T(4,128)} %copy.46), calls=%async_computation.1 | async-start | bytes 1048576 | tf_op jit(solution)/shard_map/all_to_all | solution.py:148
  73.1 6.3 %slice.77 = f32[5,16,32,480]{3,2,1,0:T(8,128)} slice(f32[5,16,32,512]{3,2,1,0:T(8,128)} %fusion.8), slice={[0:5], [0:16], [0:32], [32:512]} | slice | bytes 9830400 | tf_op jit(solution)/shard_map/slice | solution.py:150
  79.4 3.7 %all-to-all-done.1 = f32[80,256,4]{0,2,1:T(4,128)S(1)} async-done(((f32[80,256,4]{0,2,1:T(4,128)}), f32[80,256,4]{0,2,1:T(4,128)S(1)}, u32[]{:S(2)}, u32[]{:S(2)}) %all-to-all-start.1) | async-done | bytes 327712 | tf_op jit(solution)/shard_map/all_to_all | solution.py:148
  83.1 0.4 copy.48
  83.5 0.5 copy.49
  84.1 6.3 %pad_maximum_fusion.4 = f32[5,16,32,512]{3,2,1,0:T(8,128)} fusion(f32[5,16,32,480]{3,2,1,0:T(8,128)} %slice.77, f32[5,16,32,32]{3,2,1,0:T(8,128)S(1)} %copy.49), kind=kLoop, calls=%fused_computation.19 | loop fusion | flops 1310720 | bytes 10485760 | tf_op jit(solution)/shard_map/concatenate | solution.py:150
  (20 shorter events, 0.1 us)
Async XLA Ops:
  0.0 4.1 %copy-start = (f32[5,16,32,512]{3,2,1,0:T(8,128)S(1)}, f32[5,16,32,512]{3,2,1,0:T(8,128)}, u32[]{:S(2)}) copy-start(f32[5,16,32,512]{3,2,1,0:T(8,128)} %param.6) | copy-start | bytes 15728644
  7.5 16.7 %copy-start.1 = (f32[5,16,32,512]{3,2,1,0:T(8,128)}, f32[5,16,32,512]{3,2,1,0:T(8,128)S(1)}, u32[]{:S(2)}) copy-start(f32[5,16,32,512]{3,2,1,0:T(8,128)S(1)} %get-tuple-element.12) | copy-start | bytes 15728644
  7.5 16.7 %copy-start.2 = (f32[5,16,32,512]{3,2,1,0:T(8,128)}, f32[5,16,32,512]{3,2,1,0:T(8,128)S(1)}, u32[]{:S(2)}) copy-start(f32[5,16,32,512]{3,2,1,0:T(8,128)S(1)} %get-tuple-element.11) | copy-start | bytes 15728644
  8.5 23.1 %collective-permute-start = (f32[5,1,32,512]{3,2,1,0:T(8,128)}, f32[5,1,32,512]{3,2,1,0:T(8,128)S(1)}, u32[]{:S(2)}, u32[]{:S(2)}) collective-permute-start(f32[5,1,32,512]{3,2,1,0:T(8,128)} %get-tuple-element.16), channel_id=1, source_target_pairs={{8,0},{16,8},{24,16},{32,24},{40,32},{48,40},{56,48},{64,56},{72,6... | collective-permute-start | bytes 983048 | tf_op jit(solution)/shard_map/ppermute | solution.py:25
  13.6 18.0 %collective-permute-start.1 = (f32[5,1,32,512]{3,2,1,0:T(8,128)}, f32[5,1,32,512]{3,2,1,0:T(8,128)}, u32[]{:S(2)}, u32[]{:S(2)}) collective-permute-start(f32[5,1,32,512]{3,2,1,0:T(8,128)} %get-tuple-element.17), channel_id=1, source_target_pairs={{0,8},{8,16},{16,24},{24,32},{32,40},{40,48},{48,56},{56,64},{64,7... | collective-permute-start | bytes 983048 | tf_op jit(solution)/shard_map/ppermute | solution.py:23
  16.5 8.0 %collective-permute-start.2 = (f32[5,16,1,512]{3,1,2,0:T(8,128)}, f32[5,16,1,512]{3,1,2,0:T(8,128)}, u32[]{:S(2)}, u32[]{:S(2)}) collective-permute-start(f32[5,16,1,512]{3,1,2,0:T(8,128)} %copy.38), channel_id=1, source_target_pairs={{1,0},{2,1},{3,2},{4,3},{5,4},{6,5},{7,6},{0,7},{9,8},{10,9},{11,1... | collective-permute-start | bytes 491528 | tf_op jit(solution)/shard_map/ppermute | solution.py:25
  20.5 10.0 %collective-permute-start.3 = (f32[5,16,1,512]{3,1,2,0:T(8,128)}, f32[5,16,1,512]{3,1,2,0:T(8,128)}, u32[]{:S(2)}, u32[]{:S(2)}) collective-permute-start(f32[5,16,1,512]{3,1,2,0:T(8,128)} %copy.40), channel_id=1, source_target_pairs={{0,1},{1,2},{2,3},{3,4},{4,5},{5,6},{6,7},{7,0},{8,9},{9,10},{10,1... | collective-permute-start | bytes 491528 | tf_op jit(solution)/shard_map/ppermute | solution.py:23
  21.1 3.1 %copy-start.3 = (s32[16,32,512]{2,1,0:T(8,128)S(1)}, s32[16,32,512]{2,1,0:T(8,128)}, u32[]{:S(2)}) copy-start(s32[16,32,512]{2,1,0:T(8,128)} %param.7) | copy-start | bytes 3145732
  21.2 3.2 %copy-start.5 = (f32[512]{0:T(512)S(1)}, f32[512]{0:T(512)}, u32[]{:S(2)}) copy-start(f32[512]{0:T(512)} %param.9) | copy-start | bytes 6148
  21.2 3.3 %copy-start.6 = (s32[32]{0:T(128)S(1)}, s32[32]{0:T(128)}, u32[]{:S(2)}) copy-start(s32[32]{0:T(128)} %param.11) | copy-start | bytes 388
  21.2 3.4 %copy-start.7 = (f32[16]{0:T(128)S(1)}, f32[16]{0:T(128)}, u32[]{:S(2)}) copy-start(f32[16]{0:T(128)} %param.8) | copy-start | bytes 196
  21.2 10.4 %copy-start.4 = (f32[5,512]{1,0:T(8,128)S(1)}, f32[5,512]{1,0:T(8,128)}, u32[]{:S(2)}) copy-start(f32[5,512]{1,0:T(8,128)} %param.10) | copy-start | bytes 30724
  52.5 13.4 %all-to-all-start = ((f32[80,32,32]{0,1,2:T(8,128)}), f32[80,32,32]{0,1,2:T(8,128)S(1)}, u32[]{:S(2)}, u32[]{:S(2)}) async-start(f32[80,32,32]{0,1,2:T(8,128)} %copy.42), calls=%async_computation | async-start | bytes 1048576 | tf_op jit(solution)/shard_map/all_to_all | solution.py:145
  69.4 13.7 %all-to-all-start.1 = ((f32[80,256,4]{0,2,1:T(4,128)}), f32[80,256,4]{0,2,1:T(4,128)S(1)}, u32[]{:S(2)}, u32[]{:S(2)}) async-start(f32[80,256,4]{0,2,1:T(4,128)} %copy.46), calls=%async_computation.1 | async-start | bytes 1048576 | tf_op jit(solution)/shard_map/all_to_all | solution.py:148
where the time goes:
time: 90.8 us; the launch traced here: 90.3 us
  other arithmetic  34.8 us (38%)
  waiting for transfers between devices  18.3 us (20%)
  starting transfers between devices  17.5 us (19%)
  local copies, waits for them, and re-layouts  17 us (19%)
  matrix products  2.36 us (3%)
    add x1, other arithmetic, body(): updated = state + time_step * tendency  17.8 us
    all_to_all x1, waiting for transfers between devices, body(): lax.all_to_all(inner_block, 'az', split_axis=2, concat_axis=1, tiled=True)  9.82 us
    ppermute x2, starting transfers between devices, extended(): lax.ppermute(head, axis, [((i + 1) % count, i) for i in range(ends)])  8.4 us
    concatenate x1, other arithmetic, body(): return jnp.concatenate([filtered, updated[..., CYCLE:]], axis=3)  6.26 us
    slice x1, local copies, waits for them, and re-layouts, body(): return jnp.concatenate([filtered, updated[..., CYCLE:]], axis=3)  6.26 us
    ppermute x2, waiting for transfers between devices, extended(): lax.ppermute(tail, axis, [(i, (i + 1) % count) for i in range(ends)])  4.8 us
    all_to_all x1, starting transfers between devices, body(): lax.all_to_all(turned, 'az', split_axis=1, concat_axis=2, tiled=True)  3.71 us
    all_to_all x1, waiting for transfers between devices, body(): lax.all_to_all(turned, 'az', split_axis=1, concat_axis=2, tiled=True)  3.71 us
  transfers between devices with their start and end apart: 6, of which 3 were waited for; matrix products, arithmetic and copies ran while one was open for 16% of the time, Pallas kernels for 0%

commit v1 on v0

v1 whole, which is shorter than its diff:
```python
import jax
import jax.numpy as jnp
import numpy as np
from jax import lax
from jax.experimental import pallas as pl
from jax.experimental.pallas import tpu as pltpu
from jax.sharding import PartitionSpec as P

NT = 256
CYCLE = 32
NR = 512
PL_DEV = 16
CELLS = 32
TOP = 32
LT = NR // 128

time_step = 0.02
sponge_rate = 4.0

ROWS = 88
BACK = 80


def tables():
    cell = np.arange(NT)
    cos = np.cos(2 * np.pi * ((np.arange(TOP + 1)[:, None] * cell[None]) % NT) / NT)
    sin = np.sin(2 * np.pi * ((np.arange(1, TOP + 1)[:, None] * cell[None]) % NT) / NT)
    whole = np.zeros((80, NT), np.float32)
    whole[: TOP + 1] = cos
    whole[TOP + 1 : 2 * TOP + 1] = sin
    high = whole.astype(jnp.bfloat16)
    low = (whole - high.astype(np.float32)).astype(jnp.bfloat16)
    fwd = np.concatenate([high, low], 0)
    inv = np.concatenate([high.T, low.T, high.T], 1)
    return fwd, inv


def prims(st):
    density, mx, mr, ms, energy = st
    inv = 1.0 / density
    u = mx * inv
    v = mr * inv
    w = ms * inv
    a = mx * u
    b = mr * v
    c = ms * w
    pressure = 0.4 * (energy - 0.5 * (a + b + c))
    return u, v, w, a, b, c, pressure, energy + pressure


def kernel(
    state, sponge, inv_dr, target, fwd_t, inv_t, inv_dx, cutoff, out,
    ST, FX, PART, SP, TG, IDR, CC, TT, LC, SB, RB, SB2, R2, WT,
    load_sem, small_sem, ax_send, ax_recv, sw_send, sw_recv, send1, recv1, send2, recv2,
):
    gx = lax.axis_index("gx")
    az = lax.axis_index("az")
    n_gx = lax.axis_size("gx")
    n_az = lax.axis_size("az")
    up, down = lax.rem(gx + 1, n_gx), lax.rem(gx + n_gx - 1, n_gx)
    east, west = lax.rem(az + 1, n_az), lax.rem(az + n_az - 1, n_az)

    barrier = pltpu.get_barrier_semaphore()
    for k in range(1, n_az):
        pl.semaphore_signal(barrier, inc=1, device_id={"az": lax.rem(az + k, n_az)})
    for g in (up, down):
        pl.semaphore_signal(barrier, inc=1, device_id={"gx": g})

    def lanes(l):
        return pl.ds(l * 128, 128)

    loads = []
    for l in range(LT):
        loads.append(
            (
                pltpu.make_async_copy(
                    state.at[:, :, :, lanes(l)],
                    ST.at[l, :, 1:17, 8:40, :],
                    load_sem.at[2 * l],
                ),
                pltpu.make_async_copy(
                    sponge.at[:, :, lanes(l)], SP.at[l], load_sem.at[2 * l + 1]
                ),
            )
        )
    small = [
        pltpu.make_async_copy(inv_dr, IDR, small_sem.at[0]),
        pltpu.make_async_copy(target, TG, small_sem.at[1]),
        pltpu.make_async_copy(fwd_t, CC, small_sem.at[2]),
        pltpu.make_async_copy(inv_t, TT, small_sem.at[3]),
    ]
    for c in loads[0]:
        c.start()
    small[0].start()
    small[1].start()

    def axial(l, side):
        plane = 15 if side == 0 else 0
        slot = 0 if side == 0 else 17
        return pltpu.make_async_remote_copy(
            src_ref=state.at[:, plane : plane + 1, :, lanes(l)],
            dst_ref=ST.at[l, :, slot : slot + 1, 8:40, :],
            send_sem=ax_send.at[l, side],
            recv_sem=ax_recv.at[l, side],
            device_id={"gx": up if side == 0 else down},
        )

    def swirl(l, side):
        row = 31 if side == 0 else 0
        slot = 7 if side == 0 else 40
        return pltpu.make_async_remote_copy(
            src_ref=state.at[:, :, row : row + 1, lanes(l)],
            dst_ref=ST.at[l, :, 1:17, slot : slot + 1, :],
            send_sem=sw_send.at[l, side],
            recv_sem=sw_recv.at[l, side],
            device_id={"az": east if side == 0 else west},
        )

    axials = [[axial(l, s) for s in range(2)] for l in range(LT)]
    swirls = [[swirl(l, s) for s in range(2)] for l in range(LT)]

    lane = lax.broadcasted_iota(jnp.int32, (8, 128), 1)
    row = lax.broadcasted_iota(jnp.int32, (8, 128), 0)

    small[0].wait()
    small[1].wait()
    for l in range(LT):
        j = lane + l * 128
        jf = j.astype(jnp.float32)
        radius = 1.0 + 4.0 * jf / NR
        after = 1.0 + 4.0 * (jf + 1.0) / NR
        before = 1.0 + 4.0 * (jf - 1.0) / NR
        inv_r = 1.0 / radius
        rr = (0.5 * time_step) * jnp.broadcast_to(IDR[:, l * 128 : (l + 1) * 128], (8, 128)) * inv_r
        LC[0, l] = jnp.where(j == NR - 1, 0.0, rr * after)
        LC[1, l] = jnp.where(j == 0, 0.0, rr * before)
        LC[2, l] = (time_step * NT / (4.0 * np.pi)) * inv_r
        LC[3, l] = time_step * inv_r
        for f in range(5):
            LC[4 + f, l] = jnp.broadcast_to(TG[f : f + 1, l * 128 : (l + 1) * 128], (8, 128))

    cut = jnp.zeros((8, 128), jnp.int32)
    for j in range(CYCLE):
        cut = jnp.where((lane & (CYCLE - 1)) == j, cutoff[j], cut)
    for b in range(10):
        k = row + 8 * b
        mode = jnp.where(k > TOP, k - TOP, k)
        kept = (mode <= cut) & (k <= 2 * TOP)
        WT[8 * b : 8 * b + 8] = jnp.where(kept, jnp.where(k == 0, 1.0 / NT, 2.0 / NT), 0.0)

    zero = jnp.zeros((8, 128), jnp.float32)
    SWIRL = (7, 2, 4, 5, 6)

    def clear(p, _):
        for c in SWIRL:
            FX[0, c, p, 0:8] = zero
            FX[0, c, p, 40:48] = zero
        return 0

    lax.fori_loop(1, 17, clear, 0)
    for e in range(8):
        SB[e, 80:88] = zero

    pl.semaphore_wait(barrier, n_az + 1)
    for s in range(2):
        axials[0][s].start()
    for l in range(1, LT):
        for c in loads[l]:
            c.start()
    small[2].start()
    small[3].start()
    for l in range(1, LT):
        for s in range(2):
            axials[l][s].start()

    def axial_fluxes(l, p, r, st):
        density, mx, mr, ms, energy = st
        u, v, w, a, b, c, pressure, h = prims(st)
        FX[l, 0, p, r] = a + pressure
        a2 = mr * u
        FX[l, 1, p, r] = a2
        FX[l, 2, p, r] = ms * u
        FX[l, 3, p, r] = h * u
        return v, w, b, c, pressure, h, a2

    def swirl_fluxes(l, p, r, mr, ms, w, c, pressure, h):
        s2 = mr * w
        s3 = c + pressure
        FX[l, 4, p, r] = s2
        FX[l, 5, p, r] = s3
        FX[l, 6, p, r] = h * w
        FX[l, 7, p, r] = ms
        return s2, s3

    def block(ls, p, g):
        r = pl.ds(8 + 8 * g, 8)
        states, radials, sources = [], [], []
        for l in ls:
            st = [ST[l, f, p, r] for f in range(5)]
            mr, ms = st[2], st[3]
            v, w, b, c, pressure, h, a2 = axial_fluxes(l, p, r, st)
            s2, s3 = swirl_fluxes(l, p, r, mr, ms, w, c, pressure, h)
            states.append(st)
            radials.append((mr, a2, b + pressure, s2, h * v))
            sources.append((s2, s3))
        fwd = [[pltpu.roll(x, 127, 1) for x in rs] for rs in radials]
        bwd = [[pltpu.roll(x, 1, 1) for x in rs] for rs in radials]
        for i, l in enumerate(ls):
            level = SP[l, p - 1, pl.ds(8 * g, 8)].astype(jnp.float32) * (time_step * sponge_rate)
            for f in range(5):
                ahead, behind = fwd[i][f], bwd[i][f]
                if i + 1 < len(ls):
                    ahead = jnp.where(lane == 127, fwd[i + 1][f], ahead)
                if i > 0:
                    behind = jnp.where(lane == 0, bwd[i - 1][f], behind)
                x = states[i][f]
                part = x - level * (x - LC[4 + f, l]) - (ahead * LC[0, l] - behind * LC[1, l])
                if f == 2:
                    part = part + LC[3, l] * sources[i][1]
                if f == 3:
                    part = part - LC[3, l] * sources[i][0]
                PART[l, f, p - 1, pl.ds(8 * g, 8)] = part

    def edge_plane(l, p):
        for g in range(4):
            r = pl.ds(8 + 8 * g, 8)
            axial_fluxes(l, p, r, [ST[l, f, p, r] for f in range(5)])

    def second(l, f, p, g, ahead, behind):
        r = pl.ds(8 + 8 * g, 8)
        if f == 0:
            above, below = ST[l, 1, p + 1, r], ST[l, 1, p - 1, r]
        else:
            above, below = FX[l, f - 1, p + 1, r], FX[l, f - 1, p - 1, r]
        c = SWIRL[f]
        turn = FX[l, c, p, pl.ds(9 + 8 * g, 8)] - FX[l, c, p, pl.ds(7 + 8 * g, 8)]
        x = PART[l, f, p - 1, pl.ds(8 * g, 8)]
        return x - (above * ahead - below * behind) - LC[2, l] * turn

    def steps_of(p):
        step = (0.5 * time_step) * inv_dx[p - 1]
        none = jnp.float32(0.0)
        ahead = jnp.where((p == 16) & (gx == n_gx - 1), none, step)
        behind = jnp.where((p == 1) & (gx == 0), none, step)
        return ahead, behind

    def pack(xs):
        got = xs[0]
        for i in range(1, 4):
            got = jnp.where(lane >= 32 * i, pltpu.roll(xs[i], 32 * i, 1), got)
        return got

    def forth(e):
        return pltpu.make_async_remote_copy(
            src_ref=SB.at[e], dst_ref=RB.at[az], send_sem=send1.at[e], recv_sem=recv1.at[az],
            device_id={"az": e},
        )

    def group(q):
        planes = [lax.rem(1 + 4 * q + i, 16) + 1 for i in range(4)]
        coefs = [steps_of(p) for p in planes]
        for f in range(5):
            xs = [pack([second(0, f, p, g, *s) for p, s in zip(planes, coefs)]) for g in range(4)]
            c = SWIRL[f]
            first = pack([FX[0, c, p, 8:16] for p in planes]) * pack([-LC[2, 0]] * 4)
            last = pack([FX[0, c, p, 32:40] for p in planes]) * pack([LC[2, 0]] * 4)
            if f != 2:
                e = q if f < 2 else q + 4
                s = f if f < 2 else f - 3
                for g in range(4):
                    SB[e, 32 * s + 8 * g : 32 * s + 8 * g + 8] = xs[g]
                SB[e, 80 + 2 * s : 81 + 2 * s] = first[0:1]
                SB[e, 81 + 2 * s : 82 + 2 * s] = last[7:8]
            else:
                half = lane < 64
                for g in range(2):
                    SB[q, 64 + 8 * g : 72 + 8 * g] = jnp.where(half, xs[g], pltpu.roll(xs[g + 2], 64, 1))
                    SB[q + 4, 64 + 8 * g : 72 + 8 * g] = jnp.where(half, pltpu.roll(xs[g], 64, 1), xs[g + 2])
                low = lax.broadcasted_iota(jnp.int32, (1, 128), 1) < 64
                top, end = first[0:1], last[7:8]
                SB[q, 84:85] = jnp.where(low, end, pltpu.roll(first, 64, 1)[0:1])
                SB[q + 4, 84:85] = jnp.where(low, pltpu.roll(last, 64, 1)[7:8], top)
        for y in range(2):
            e = q + 4 * y

            @pl.when(e != az)
            def _():
                forth(e).start()

            @pl.when(e == az)
            def _():
                RB[e] = SB[e]

    for c in loads[0]:
        c.wait()

    def inner(p, _):
        for g in range(4):
            block([0], p, g)
        return 0

    lax.fori_loop(1, 17, inner, 0)

    def early(q, _):
        group(q)
        return 0

    lax.fori_loop(0, 3, early, 0)
    for s in range(2):
        axials[0][s].wait_recv()
    edge_plane(0, 0)
    edge_plane(0, 17)
    group(jnp.int32(3))
    for l in range(LT):
        for s in range(2):
            swirls[l][s].start()

    for l in range(1, LT):
        for c in loads[l]:
            c.wait()

    def outer(p, _):
        for g in range(4):
            block(list(range(LT)), p, g)
        return 0

    lax.fori_loop(1, 17, outer, 0)

    small[2].wait()
    small[3].wait()
    for s in range(8):

        @pl.when(s != az)
        def _():
            pltpu.make_async_remote_copy(
                src_ref=SB.at[s], dst_ref=RB.at[s], send_sem=send1.at[s], recv_sem=recv1.at[s],
                device_id={"az": jnp.int32(s)},
            ).wait_recv()

    low1 = lax.broadcasted_iota(jnp.int32, (1, 128), 1) < 64
    for d in range(8):
        prev, nxt = (d + 7) % 8, (d + 1) % 8
        for s in range(2):
            RB[d, 32 * s : 32 * s + 1] += RB[prev, 81 + 2 * s : 82 + 2 * s]
            RB[d, 32 * s + 31 : 32 * s + 32] += RB[nxt, 80 + 2 * s : 81 + 2 * s]
        RB[d, 64:65] += jnp.where(low1, RB[prev, 84:85], 0.0)
        RB[d, 79:80] += jnp.where(low1, 0.0, RB[nxt, 84:85])
    half16 = lax.broadcasted_iota(jnp.int32, (16, 128), 1) < 64
    for s in range(3):
        if s < 2:
            xs = [RB[d, 32 * s : 32 * s + 32] for d in range(8)]
        else:
            xs = []
            for d in range(8):
                t = RB[d, 64:80]
                xs += [t, pltpu.roll(t, 64, 1)]
        x = jnp.concatenate(xs, 0)
        high = x.astype(jnp.bfloat16)
        low = (x - high.astype(jnp.float32)).astype(jnp.bfloat16)
        both = jnp.dot(CC[...], high, preferred_element_type=jnp.float32)
        coef = both[0:80] + both[80:160] + jnp.dot(CC[0:80], low, preferred_element_type=jnp.float32)
        z = coef * WT[...]
        zh = z.astype(jnp.bfloat16)
        zl = (z - zh.astype(jnp.float32)).astype(jnp.bfloat16)
        y = jnp.dot(TT[...], jnp.concatenate([zh, zh, zl], 0), preferred_element_type=jnp.float32)
        for d in range(8):
            yd = y[32 * d : 32 * d + 32]
            if s < 2:
                SB2[d, 32 * s : 32 * s + 32] = yd
            else:
                SB2[d, 64:80] = jnp.where(half16, yd[0:16], pltpu.roll(yd[16:32], 64, 1))

    def back(d, src):
        return pltpu.make_async_remote_copy(
            src_ref=SB2.at[d], dst_ref=R2.at[src], send_sem=send2.at[d], recv_sem=recv2.at[src],
            device_id={"az": jnp.int32(d)},
        )

    for d in range(8):

        @pl.when(d != az)
        def _():
            back(d, az).start()

        @pl.when(d == az)
        def _():
            R2[d] = SB2[d]

    for l in range(LT):
        for s in range(2):
            if l > 0:
                axials[l][s].wait_recv()
            swirls[l][s].wait_recv()
    for l in range(1, LT):
        edge_plane(l, 0)
        edge_plane(l, 17)

    def pads(p, _):
        for l in range(LT):
            for r0 in (0, 40):
                r = pl.ds(r0, 8)
                st = [ST[l, f, p, r] for f in range(5)]
                u, v, w, a, b, c, pressure, h = prims(st)
                FX[l, 2, p, r] = st[3] * u
                swirl_fluxes(l, p, r, st[2], st[3], w, c, pressure, h)
        return 0

    lax.fori_loop(1, 17, pads, 0)

    def finish(p, _):
        ahead, behind = steps_of(p)
        for l in range(LT):
            for f in range(5):
                for g in range(4):
                    out[f, p - 1, 8 * g : 8 * g + 8, l * 128 : (l + 1) * 128] = second(l, f, p, g, ahead, behind)
        return 0

    lax.fori_loop(1, 17, finish, 0)

    for s in range(8):

        @pl.when(s != az)
        def _():
            back(s, s).wait_recv()

    def merge(q, _):
        for i in range(4):
            p = lax.rem(1 + 4 * q + i, 16)
            for f in range(5):
                for g in range(4):
                    if f != 2:
                        e = q if f < 2 else q + 4
                        s = f if f < 2 else f - 3
                        x = R2[e, 32 * s + 8 * g : 32 * s + 8 * g + 8]
                        base = 32 * i
                    else:
                        e = q if i < 2 else q + 4
                        x = R2[e, 64 + 8 * (g % 2) : 72 + 8 * (g % 2)]
                        base = 32 * (i % 2) + 64 * (g // 2)
                    if base:
                        x = pltpu.roll(x, 128 - base, 1)
                    old = out[f, p, 8 * g : 8 * g + 8, 0:128]
                    out[f, p, 8 * g : 8 * g + 8, 0:128] = jnp.where(lane < 32, x, old)
        return 0

    lax.fori_loop(0, 4, merge, 0)

    for l in range(LT):
        for s in range(2):
            axials[l][s].wait_send()
            swirls[l][s].wait_send()
    for e in range(8):

        @pl.when(e != az)
        def _():
            forth(jnp.int32(e)).wait_send()
            back(e, az).wait_send()


def solution(mesh):
    fwd, inv = tables()

    def body(state, sponge_level, inv_dx, inv_dr, target, cutoff):
        f32 = jnp.float32
        hbm = pl.BlockSpec(memory_space=pl.ANY)
        smem = pl.BlockSpec(memory_space=pltpu.SMEM)
        dma = pltpu.SemaphoreType.DMA
        return pl.pallas_call(
            kernel,
            out_shape=jax.ShapeDtypeStruct(state.shape, f32),
            in_specs=[hbm] * 6 + [smem] * 2,
            out_specs=pl.BlockSpec(memory_space=pltpu.VMEM),
            scratch_shapes=[
                pltpu.VMEM((LT, 5, 18, 48, 128), f32),
                pltpu.VMEM((LT, 8, 18, 48, 128), f32),
                pltpu.VMEM((LT, 5, 16, 32, 128), f32),
                pltpu.VMEM((LT, 16, 32, 128), jnp.int32),
                pltpu.VMEM((5, NR), f32),
                pltpu.VMEM((1, NR), f32),
                pltpu.VMEM(fwd.shape, jnp.bfloat16),
                pltpu.VMEM(inv.shape, jnp.bfloat16),
                pltpu.VMEM((9, LT, 8, 128), f32),
                pltpu.VMEM((8, ROWS, 128), f32),
                pltpu.VMEM((8, ROWS, 128), f32),
                pltpu.VMEM((8, BACK, 128), f32),
                pltpu.VMEM((8, BACK, 128), f32),
                pltpu.VMEM((80, 128), f32),
                dma((2 * LT,)),
                dma((4,)),
                dma((LT, 2)),
                dma((LT, 2)),
                dma((LT, 2)),
                dma((LT, 2)),
                dma((8,)),
                dma((8,)),
                dma((8,)),
                dma((8,)),
            ],
            compiler_params=pltpu.CompilerParams(collective_id=0, has_side_effects=True, vmem_limit_bytes=52 << 20),
        )(state, sponge_level, inv_dr.reshape(1, NR), target, jnp.asarray(fwd), jnp.asarray(inv), inv_dx, cutoff)

    return jax.shard_map(
        body,
        mesh=mesh,
        in_specs=(P(None, "gx", "az", None), P("gx", "az", None), P("gx"), P(), P(), P()),
        out_specs=P(None, "gx", "az", None),
        check_vma=False,
    )
```

time: 90.8 us -> 45 us (0.50)
  the two profiles are of different devices: /device:TPU:1 before, /device:TPU:26 now
where the time goes in v1:
time: 45 us; the launch traced here: 44.7 us
  Pallas kernels  33 us (73%)
  local copies, waits for them, and re-layouts  11.6 us (26%)
    pallas_call x1, Pallas kernels, body(): pl.pallas_call(kernel, out_shape=jax.ShapeDtypeStruct(state.shape, f32),...  33 us
    unnamed x15, local copies, waits for them, and re-layouts  11.6 us

profile of v1, /device:TPU:26, one launch (start us, length us, event | category | flops | bytes accessed | tf_op | source)
XLA Modules:
  0.0 44.7 jit_solution(18129691630183513082)
XLA Ops:
  0.0 0.0 copy-start
  0.0 1.2 %copy-done = s32[16,32,512]{2,1,0:T(8,128)S(1)} copy-done((s32[16,32,512]{2,1,0:T(8,128)S(1)}, s32[16,32,512]{2,1,0:T(8,128)}, u32[]{:S(2)}) %copy-start) | copy-done | bytes 1048600
  1.2 0.0 copy-start.1
  1.2 0.9 %copy-done.1 = bf16[256,240]{1,0:T(8,128)(2,1)S(1)} copy-done((bf16[256,240]{1,0:T(8,128)(2,1)S(1)}, bf16[256,240]{1,0:T(8,128)(2,1)}, u32[]{:S(2)}) %copy-start.1) | copy-done | bytes 122904
  2.1 0.0 copy-start.2
  2.1 0.9 %copy-done.2 = bf16[160,256]{1,0:T(8,128)(2,1)S(1)} copy-done((bf16[160,256]{1,0:T(8,128)(2,1)S(1)}, bf16[160,256]{1,0:T(8,128)(2,1)}, u32[]{:S(2)}) %copy-start.2) | copy-done | bytes 81944
  3.0 0.0 copy-start.3
  3.0 0.7 %copy-done.3 = f32[5,512]{1,0:T(8,128)S(1)} copy-done((f32[5,512]{1,0:T(8,128)S(1)}, f32[5,512]{1,0:T(8,128)}, u32[]{:S(2)}) %copy-start.3) | copy-done | bytes 10264
  3.7 0.0 copy-start.4
  3.7 0.7 %copy-done.4 = f32[512]{0:T(512)S(1)} copy-done((f32[512]{0:T(512)S(1)}, f32[512]{0:T(512)}, u32[]{:S(2)}) %copy-start.4) | copy-done | bytes 2072
  4.4 0.0 copy-start.5
  4.4 0.7 %copy-done.5 = f32[16]{0:T(128)S(1)} copy-done((f32[16]{0:T(128)S(1)}, f32[16]{0:T(128)}, u32[]{:S(2)}) %copy-start.5) | copy-done | bytes 88
  5.1 0.0 copy-start.6
  5.1 0.7 %copy-done.6 = s32[32]{0:T(128)S(1)} copy-done((s32[32]{0:T(128)S(1)}, s32[32]{0:T(128)}, u32[]{:S(2)}) %copy-start.6) | copy-done | bytes 152
  5.7 33.0 %shard_map.82 = f32[5,16,32,512]{3,2,1,0:T(8,128)} custom-call(f32[5,16,32,512]{3,2,1,0:T(8,128)} %state.1, s32[16,32,512]{2,1,0:T(8,128)S(1)} %copy-done, f32[1,512]{1,0:T(1,128)S(1)} %bitcast.1, f32[5,512]{1,0:T(8,128)S(1)} %copy-done.3, bf16[160,256]{1,0:T(8,128)(2,1)S(1)} %copy-done.2, bf16[256,240]{1,0:T(8,128)(2,1)S(1)} %copy-done.1, f32[16]{0:T(128)S(1)} %copy-done.5, ...), custom_call_target="tpu_custom_call" | custom-call | tf_op jit(solution)/shard_map/pallas_call | solution.py:468
  38.8 5.9 %copy.10 = f32[5,16,32,512]{3,2,1,0:T(8,128)} copy(f32[5,16,32,512]{3,2,1,0:T(8,128)} %shard_map.82) | data formatting | bytes 10485760
Async XLA Ops:
  0.0 1.2 %copy-start = (s32[16,32,512]{2,1,0:T(8,128)S(1)}, s32[16,32,512]{2,1,0:T(8,128)}, u32[]{:S(2)}) copy-start(s32[16,32,512]{2,1,0:T(8,128)} %sponge.1) | copy-start | bytes 3145732
  1.2 0.9 %copy-start.1 = (bf16[256,240]{1,0:T(8,128)(2,1)S(1)}, bf16[256,240]{1,0:T(8,128)(2,1)}, u32[]{:S(2)}) copy-start(bf16[256,240]{1,0:T(8,128)(2,1)} %constant.5.clone.inv_t) | copy-start | bytes 368644
  2.1 0.9 %copy-start.2 = (bf16[160,256]{1,0:T(8,128)(2,1)S(1)}, bf16[160,256]{1,0:T(8,128)(2,1)}, u32[]{:S(2)}) copy-start(bf16[160,256]{1,0:T(8,128)(2,1)} %constant.4.clone.fwd_t) | copy-start | bytes 245764
  3.0 0.7 %copy-start.3 = (f32[5,512]{1,0:T(8,128)S(1)}, f32[5,512]{1,0:T(8,128)}, u32[]{:S(2)}) copy-start(f32[5,512]{1,0:T(8,128)} %target.1) | copy-start | bytes 30724
  3.7 0.7 %copy-start.4 = (f32[512]{0:T(512)S(1)}, f32[512]{0:T(512)}, u32[]{:S(2)}) copy-start(f32[512]{0:T(512)} %param.11) | copy-start | bytes 6148
  4.4 0.7 %copy-start.5 = (f32[16]{0:T(128)S(1)}, f32[16]{0:T(128)}, u32[]{:S(2)}) copy-start(f32[16]{0:T(128)} %inv_dx.1) | copy-start | bytes 196
  5.1 0.7 %copy-start.6 = (s32[32]{0:T(128)S(1)}, s32[32]{0:T(128)}, u32[]{:S(2)}) copy-start(s32[32]{0:T(128)} %cutoff.1) | copy-start | bytes 388

commit v2 on v1

v2 whole, which is shorter than its diff:
```python
import jax
import jax.numpy as jnp
import numpy as np
from jax import lax
from jax.experimental import pallas as pl
from jax.experimental.pallas import tpu as pltpu
from jax.sharding import PartitionSpec as P

NT = 256
CYCLE = 32
NR = 512
PL_DEV = 16
CELLS = 32
TOP = 32
LT = NR // 128

time_step = 0.02
sponge_rate = 4.0

ROWS = 88
BACK = 80
N1 = 12


def tables():
    cell = np.arange(NT)
    cos = np.cos(2 * np.pi * ((np.arange(TOP + 1)[:, None] * cell[None]) % NT) / NT)
    sin = np.sin(2 * np.pi * ((np.arange(1, TOP + 1)[:, None] * cell[None]) % NT) / NT)
    whole = np.zeros((80, NT), np.float32)
    whole[: TOP + 1] = cos
    whole[TOP + 1 : 2 * TOP + 1] = sin
    high = whole.astype(jnp.bfloat16)
    low = (whole - high.astype(np.float32)).astype(jnp.bfloat16)
    fwd = np.concatenate([high, low], 0)
    inv = np.concatenate([high.T, low.T, high.T], 1)
    return fwd, inv


def prims(st):
    density, mx, mr, ms, energy = st
    inv = 1.0 / density
    u = mx * inv
    v = mr * inv
    w = ms * inv
    a = mx * u
    b = mr * v
    c = ms * w
    pressure = 0.4 * (energy - 0.5 * (a + b + c))
    return u, v, w, a, b, c, pressure, energy + pressure


def kernel(
    state, sponge, inv_dr, target, fwd_t, inv_t, inv_dx_in, cutoff_in, out, R2,
    ST, FX, PART, SP, TG, IDR, CC, TT, LC, PC, PI, FA, SI, SB, RB, SB2, HS, HR, RL, WT, inv_dx, cutoff,
    load_sem, small_sem, ax_send, ax_recv, sw_send, sw_recv, send1, recv1, send2, recv2, hs_send, hs_recv,
    rl_send, rl_recv,
):
    gx = lax.axis_index("gx")
    az = lax.axis_index("az")
    n_gx = lax.axis_size("gx")
    n_az = lax.axis_size("az")
    has_up, has_down = gx < n_gx - 1, gx > 0
    up, down = lax.rem(gx + 1, n_gx), lax.rem(gx + n_gx - 1, n_gx)
    east, west = lax.rem(az + 1, n_az), lax.rem(az + n_az - 1, n_az)
    partner = lax.rem(az + 4, n_az)
    mid = n_gx // 2
    up_relay = [mid - 1 - 2 * l for l in range(LT)]
    down_relay = [n_gx - 1 - 2 * l for l in range(LT)]
    first_x, last_x = lax.rem(az, 4) == 0, lax.rem(az, 4) == 3

    def lanes(l):
        return pl.ds(l * 128, 128)

    loads = []
    for l in range(LT):
        loads.append(
            (
                pltpu.make_async_copy(
                    state.at[:, :, :, lanes(l)],
                    ST.at[l, :, 1:17, 8:40, :],
                    load_sem.at[2 * l],
                ),
                pltpu.make_async_copy(
                    sponge.at[:, :, lanes(l)], SP.at[l], load_sem.at[2 * l + 1]
                ),
            )
        )
    small = [
        pltpu.make_async_copy(inv_dr, IDR, small_sem.at[0]),
        pltpu.make_async_copy(target, TG, small_sem.at[1]),
        pltpu.make_async_copy(fwd_t, CC, small_sem.at[2]),
        pltpu.make_async_copy(inv_t, TT, small_sem.at[3]),
        pltpu.make_async_copy(inv_dx_in, inv_dx, small_sem.at[4]),
        pltpu.make_async_copy(cutoff_in, cutoff, small_sem.at[5]),
    ]
    for k in (0, 1, 4, 5):
        small[k].start()
    for c in loads[0]:
        c.start()
    barrier = pltpu.get_barrier_semaphore()
    for k in range(1, n_az):
        pl.semaphore_signal(barrier, inc=1, device_id={"az": lax.rem(az + k, n_az)})
    for there, g, holds in ((has_down, down, first_x), (has_up, up, last_x)):

        @pl.when(there)
        def _():
            pl.semaphore_signal(barrier, inc=1, device_id={"gx": g})

        @pl.when(there & holds)
        def _():
            for d in range(8):
                pl.semaphore_signal(barrier, inc=1, device_id={"gx": g, "az": jnp.int32(d)})

    relays = 0
    for l in range(LT):
        for g, to in (
            (up_relay[l], mid - 1), (mid, up_relay[l]), (down_relay[l], mid), (mid - 1, down_relay[l])
        ):
            if g != to:

                @pl.when(gx == g)
                def _():
                    pl.semaphore_signal(barrier, inc=1, device_id={"gx": jnp.int32(to), "az": partner})

                relays = relays + (gx == to).astype(jnp.int32)
    greeted = n_az - 1 + 3 * has_up.astype(jnp.int32) + 3 * has_down.astype(jnp.int32) + relays


    def axial(l, side):
        plane = 15 if side == 0 else 0
        slot = 0 if side == 0 else 17
        return pltpu.make_async_remote_copy(
            src_ref=state.at[:, plane : plane + 1, :, lanes(l)],
            dst_ref=ST.at[l, :, slot : slot + 1, 8:40, :],
            send_sem=ax_send.at[l, side],
            recv_sem=ax_recv.at[l, side],
            device_id={"gx": up if side == 0 else down},
        )

    def swirl(l, side):
        row = 31 if side == 0 else 0
        slot = 7 if side == 0 else 40
        return pltpu.make_async_remote_copy(
            src_ref=state.at[:, :, row : row + 1, lanes(l)],
            dst_ref=ST.at[l, :, 1:17, slot : slot + 1, :],
            send_sem=sw_send.at[l, side],
            recv_sem=sw_recv.at[l, side],
            device_id={"az": east if side == 0 else west},
        )

    axials = [[axial(l, s) for s in range(2)] for l in range(LT)]
    swirls = [[swirl(l, s) for s in range(2)] for l in range(LT)]
    sends_to = (has_up, has_down)
    direct = (has_up & (gx != mid - 1), has_down & (gx != mid))
    gets_from = (has_down, has_up)

    lane = lax.broadcasted_iota(jnp.int32, (8, 128), 1)
    row = lax.broadcasted_iota(jnp.int32, (8, 128), 0)
    cycle = lane & (CYCLE - 1)

    def pack(xs):
        got = xs[0]
        for i in range(1, 4):
            got = jnp.where(lane >= 32 * i, pltpu.roll(xs[i], 32 * i, 1), got)
        return got

    for k in (0, 1, 4, 5):
        small[k].wait()

    def coefficients(j, spacing):
        jf = j.astype(jnp.float32)
        after = 1.0 + 4.0 * (jf + 1.0) / NR
        before = 1.0 + 4.0 * (jf - 1.0) / NR
        inv_r = 1.0 / (1.0 + 4.0 * jf / NR)
        rr = (0.5 * time_step) * spacing * inv_r
        return (
            jnp.where(j == NR - 1, 0.0, rr * after),
            jnp.where(j == 0, 0.0, rr * before),
            (time_step * NT / (4.0 * np.pi)) * inv_r,
            time_step * inv_r,
        )

    def wide(ref, f, l):
        return jnp.broadcast_to(ref[f : f + 1, l * 128 : (l + 1) * 128], (8, 128))

    for k, x in enumerate(coefficients(cycle, pack([wide(IDR, 0, 0)] * 4))):
        PC[k] = x
    for f in range(5):
        PC[4 + f] = pack([wide(TG, f, 0)] * 4)
    for q in range(4):
        x = jnp.zeros((8, 128), jnp.float32)
        for i in range(4):
            x = jnp.where(lane >= 32 * i, (0.5 * time_step) * inv_dx[4 * q + i], x)
        PC[9 + q] = x
    for l in range(LT):
        for k, x in enumerate(coefficients(lane + l * 128, wide(IDR, 0, l))):
            LC[k, l] = x
        for f in range(5):
            LC[4 + f, l] = wide(TG, f, l)

    cut = jnp.zeros((8, 128), jnp.int32)
    for j in range(CYCLE):
        cut = jnp.where(cycle == j, cutoff[j], cut)
    for b in range(10):
        k = row + 8 * b
        mode = jnp.where(k > TOP, k - TOP, k)
        kept = (mode <= cut) & (k <= 2 * TOP)
        WT[8 * b : 8 * b + 8] = jnp.where(kept, jnp.where(k == 0, 1.0 / NT, 2.0 / NT), 0.0)

    zero = jnp.zeros((8, 128), jnp.float32)
    for q in range(4):
        for c in range(5):
            SI[q, c, 0:8] = zero
            SI[q, c, 40:48] = zero
    for c in range(5):
        for g in range(4):
            FA[0, c, 8 * g : 8 * g + 8] = zero
            FA[5, c, 8 * g : 8 * g + 8] = zero
    for e in range(8):
        SB[e, 32:40] = zero

    for c in loads[0]:
        c.wait()
    for l in range(1, LT):
        for c in loads[l]:
            c.start()
    small[2].start()
    small[3].start()

    def inner(q, _):
        for g in range(4):
            r = pl.ds(8 + 8 * g, 8)
            o = pl.ds(8 * g, 8)
            raw = [[ST[0, f, 4 * q + 1 + i, r] for i in range(4)] for f in range(5)]
            st = [pack(xs) for xs in raw]
            nx = []
            for xs in raw:
                got = pltpu.roll(xs[0], 127, 1)
                for i in range(1, 4):
                    got = jnp.where(lane >= 32 * i, pltpu.roll(xs[i], 32 * i - 1, 1), got)
                nx.append(got)
            level = pack([SP[0, 4 * q + i, o] for i in range(4)]).astype(jnp.float32) * (time_step * sponge_rate)
            density, mx, mr, ms, energy = st
            u, v, w, a, b, c, pressure, h = prims(st)
            a2, a3, s2, s3 = mr * u, ms * u, mr * w, c + pressure
            for k, x in enumerate((mx, a + pressure, a2, a3, h * u)):
                FA[q + 1, k, o] = x
            for k, x in enumerate((ms, a3, s2, s3, h * w)):
                SI[q, k, r] = x
            behind = [pltpu.roll(x, 1, 1) for x in (mr, a2, b + pressure, s2, h * v)]
            nu, nv, nw, na, nb, nc, npres, nh = prims(nx)
            ahead = (nx[2], nx[1] * nv, nb + npres, nx[3] * nv, nh * nv)
            for f in range(5):
                part = st[f] - level * (st[f] - PC[4 + f]) - (ahead[f] * PC[0] - behind[f] * PC[1])
                if f == 2:
                    part = part + PC[3] * s3
                if f == 3:
                    part = part - PC[3] * s2
                PI[q, f, o] = part
        return 0

    lax.fori_loop(0, 4, inner, 0)

    def hello(side, y):
        return pltpu.make_async_remote_copy(
            src_ref=HS.at[side, y], dst_ref=HR.at[az], send_sem=hs_send.at[side, y], recv_sem=hs_recv.at[az],
            device_id={"gx": up, "az": jnp.int32(4 * y)} if side == 0 else {"gx": down, "az": jnp.int32(4 * y + 3)},
        )

    for side in range(2):
        for f in range(5):
            xs = [FA[4 if side == 0 else 1, f, 8 * g : 8 * g + 8] for g in range(4)]
            if side == 0:
                got = pltpu.roll(xs[0], 32, 1)
                for g in range(1, 4):
                    x = pltpu.roll(xs[g], 32 * (g + 1), 1) if g < 3 else xs[g]
                    got = jnp.where(lane >= 32 * g, x, got)
            else:
                got = pack(xs)
            if f == 2:
                HS[side, 0, 16:24] = got
                HS[side, 1, 16:24] = got
            else:
                s = f if f < 2 else f - 3
                HS[side, f // 3, 8 * s : 8 * s + 8] = got

    PARTS = ((0, 40), (40, 48))

    def forth(part, e):
        at, size = PARTS[part]
        return pltpu.make_async_remote_copy(
            src_ref=SB.at[e, at : at + size], dst_ref=RB.at[az, at : at + size],
            send_sem=send1.at[part, e], recv_sem=recv1.at[part, az], device_id={"az": e},
        )

    def made(q, f):
        xs = []
        for g in range(4):
            o = pl.ds(8 * g, 8)
            own = FA[q + 1, f, o]
            above = pltpu.roll(jnp.where(lane < 32, FA[q + 2, f, o], own), 96, 1)
            below = pltpu.roll(jnp.where(lane >= 96, FA[q, f, o], own), 32, 1)
            swirl_diff = SI[q, f, pl.ds(9 + 8 * g, 8)] - SI[q, f, pl.ds(7 + 8 * g, 8)]
            xs.append(PI[q, f, o] - PC[9 + q] * (above - below) - PC[2] * swirl_diff)
        return xs

    def group_a(q, _):
        for f in range(5):
            first = -PC[2] * SI[q, f, 8:16]
            last = PC[2] * SI[q, f, 32:40]
            if f != 2:
                e = q if f < 2 else q + 4
                s = f if f < 2 else f - 3
                SB[e, 32 + 2 * s : 33 + 2 * s] = first[0:1]
                SB[e, 33 + 2 * s : 34 + 2 * s] = last[7:8]
                if s == 0:
                    xs = made(q, f)
                    for g in range(4):
                        SB[e, 8 * g : 8 * g + 8] = xs[g]
            else:
                low = lax.broadcasted_iota(jnp.int32, (1, 128), 1) < 64
                SB[q, 36:37] = jnp.where(low, last[7:8], pltpu.roll(first, 64, 1)[0:1])
                SB[q + 4, 36:37] = jnp.where(low, pltpu.roll(last, 64, 1)[7:8], first[0:1])
        return 0

    def group_b(q, _):
        for f in (1, 4):
            e = q if f < 2 else q + 4
            xs = made(q, f)
            for g in range(4):
                SB[e, 40 + 8 * g : 48 + 8 * g] = xs[g]
        xs = made(q, 2)
        half = lane < 64
        for g in range(2):
            SB[q, 72 + 8 * g : 80 + 8 * g] = jnp.where(half, xs[g], pltpu.roll(xs[g + 2], 64, 1))
            SB[q + 4, 72 + 8 * g : 80 + 8 * g] = jnp.where(half, pltpu.roll(xs[g], 64, 1), xs[g + 2])
        return 0

    def sent(part):
        at, size = PARTS[part]
        for k in range(1, 8):
            forth(part, lax.rem(az + k, n_az)).start()
        RB[az, at : at + size] = SB[az, at : at + size]

    lax.fori_loop(0, 4, group_a, 0)
    pl.semaphore_wait(barrier, greeted)
    sent(0)
    for side in range(2):

        @pl.when(sends_to[side])
        def _():
            for y in range(2):
                hello(side, y).start()

    lax.fori_loop(0, 4, group_b, 0)
    sent(1)
    for l in range(LT):
        for s in range(2):
            swirls[l][s].start()
    for s in range(2):

        @pl.when(direct[s])
        def _():
            for l in range(LT):
                axials[l][s].start()

    def leg(l, side):
        plane = 15 if side == 0 else 0
        return pltpu.make_async_remote_copy(
            src_ref=state.at[:, plane : plane + 1, :, lanes(l)], dst_ref=RL,
            send_sem=ax_send.at[l, side], recv_sem=rl_recv,
            device_id={"gx": jnp.int32((up_relay if side == 0 else down_relay)[l]), "az": partner},
        )

    def relay(l, side):
        slot = 0 if side == 0 else 17
        return pltpu.make_async_remote_copy(
            src_ref=RL, dst_ref=ST.at[l, :, slot : slot + 1, 8:40, :],
            send_sem=rl_send, recv_sem=ax_recv.at[l, side],
            device_id={"gx": jnp.int32(mid if side == 0 else mid - 1), "az": partner},
        )

    starts = (gx == mid - 1, gx == mid)
    for s in range(2):

        @pl.when(starts[s])
        def _():
            for l in range(LT):
                leg(l, s).start()

    SWIRL = (7, 2, 4, 5, 6)

    def axial_fluxes(l, p, r, st):
        density, mx, mr, ms, energy = st
        u, v, w, a, b, c, pressure, h = prims(st)
        FX[l, 0, p, r] = a + pressure
        a2 = mr * u
        FX[l, 1, p, r] = a2
        FX[l, 2, p, r] = ms * u
        FX[l, 3, p, r] = h * u
        return v, w, b, c, pressure, h, a2

    def swirl_fluxes(l, p, r, mr, ms, w, c, pressure, h):
        s2 = mr * w
        s3 = c + pressure
        FX[l, 4, p, r] = s2
        FX[l, 5, p, r] = s3
        FX[l, 6, p, r] = h * w
        FX[l, 7, p, r] = ms
        return s2, s3

    def block(p, g):
        r = pl.ds(8 + 8 * g, 8)
        states, radials, sources = [], [], []
        for l in range(LT):
            st = [ST[l, f, p, r] for f in range(5)]
            mr, ms = st[2], st[3]
            v, w, b, c, pressure, h, a2 = axial_fluxes(l, p, r, st)
            s2, s3 = swirl_fluxes(l, p, r, mr, ms, w, c, pressure, h)
            states.append(st)
            radials.append((mr, a2, b + pressure, s2, h * v))
            sources.append((s2, s3))
        fwd = [[pltpu.roll(x, 127, 1) for x in rs] for rs in radials]
        bwd = [[pltpu.roll(x, 1, 1) for x in rs] for rs in radials]
        for l in range(LT):
            level = SP[l, p - 1, pl.ds(8 * g, 8)].astype(jnp.float32) * (time_step * sponge_rate)
            for f in range(5):
                ahead, behind = fwd[l][f], bwd[l][f]
                if l + 1 < LT:
                    ahead = jnp.where(lane == 127, fwd[l + 1][f], ahead)
                if l > 0:
                    behind = jnp.where(lane == 0, bwd[l - 1][f], behind)
                x = states[l][f]
                part = x - level * (x - LC[4 + f, l]) - (ahead * LC[0, l] - behind * LC[1, l])
                if f == 2:
                    part = part + LC[3, l] * sources[l][1]
                if f == 3:
                    part = part - LC[3, l] * sources[l][0]
                PART[l, f, p - 1, pl.ds(8 * g, 8)] = part

    for l in range(1, LT):
        for c in loads[l]:
            c.wait()

    def outer(p, _):
        for g in range(4):
            block(p, g)
        return 0

    lax.fori_loop(1, N1, outer, 0)

    small[2].wait()
    small[3].wait()

    def arrived(part):
        at, size = PARTS[part]
        for k in range(1, 8):
            s = lax.rem(az + k, n_az)
            pltpu.make_async_remote_copy(
                src_ref=SB.at[s, at : at + size], dst_ref=RB.at[s, at : at + size],
                send_sem=send1.at[part, s], recv_sem=recv1.at[part, s], device_id={"az": s},
            ).wait_recv()

    def neighbours():
        for side in range(2):

            @pl.when(gets_from[side] & (first_x if side == 0 else last_x))
            def _():
                for d in range(8):
                    pltpu.make_async_remote_copy(
                        src_ref=HS.at[0, 0], dst_ref=HR.at[d], send_sem=hs_send.at[0, 0], recv_sem=hs_recv.at[d],
                        device_id={"gx": up},
                    ).wait_recv()

    def edges(part):
        for side in range(2):

            @pl.when(gets_from[side] & (first_x if side == 0 else last_x))
            def _():
                scale = (0.5 * time_step) * inv_dx[0] if side == 0 else (-0.5 * time_step) * inv_dx[PL_DEV - 1]
                for d in range(8):
                    for s in (0,) if part == 0 else (1, 2):
                        x = HR[d, 8 * s : 8 * s + 8] * scale
                        for g in range(4):
                            if s < 2:
                                to, base = 40 * s + 8 * g, 0 if side == 0 else 96
                            else:
                                to, base = 72 + 8 * (g % 2), 64 * (g // 2) + (0 if side == 0 else 32)
                            here = (lane >= base) & (lane < base + 32)
                            if s == 2:
                                here = here & (az == (0 if side == 0 else 7))
                            y = pltpu.roll(x, (base - 32 * g) % 128, 1) if (base - 32 * g) % 128 else x
                            RB[d, to : to + 8] += jnp.where(here, y, 0.0)

        low1 = lax.broadcasted_iota(jnp.int32, (1, 128), 1) < 64
        for d in range(8):
            prev, nxt = (d + 7) % 8, (d + 1) % 8
            s = part
            RB[d, 40 * s : 40 * s + 1] += RB[prev, 33 + 2 * s : 34 + 2 * s]
            RB[d, 40 * s + 31 : 40 * s + 32] += RB[nxt, 32 + 2 * s : 33 + 2 * s]
            if part == 1:
                RB[d, 72:73] += jnp.where(low1, RB[prev, 36:37], 0.0)
                RB[d, 87:88] += jnp.where(low1, 0.0, RB[nxt, 36:37])

    half16 = lax.broadcasted_iota(jnp.int32, (16, 128), 1) < 64
    BACKS = ((0, 32), (32, 48))

    def filtered(part):
        for s in (0,) if part == 0 else (1, 2):
            if s < 2:
                xs = [RB[d, 40 * s : 40 * s + 32] for d in range(8)]
            else:
                xs = []
                for d in range(8):
                    t = RB[d, 72:88]
                    xs += [t, pltpu.roll(t, 64, 1)]
            x = jnp.concatenate(xs, 0)
            high = x.astype(jnp.bfloat16)
            low = (x - high.astype(jnp.float32)).astype(jnp.bfloat16)
            both = jnp.dot(CC[...], high, preferred_element_type=jnp.float32)
            coef = both[0:80] + both[80:160] + jnp.dot(CC[0:80], low, preferred_element_type=jnp.float32)
            z = coef * WT[...]
            zh = z.astype(jnp.bfloat16)
            zl = (z - zh.astype(jnp.float32)).astype(jnp.bfloat16)
            y = jnp.dot(TT[...], jnp.concatenate([zh, zh, zl], 0), preferred_element_type=jnp.float32)
            for d in range(8):
                yd = y[32 * d : 32 * d + 32]
                if s < 2:
                    SB2[d, 32 * s : 32 * s + 32] = yd
                else:
                    SB2[d, 64:80] = jnp.where(half16, yd[0:16], pltpu.roll(yd[16:32], 64, 1))

    def back(part, d, src):
        at, size = BACKS[part]
        return pltpu.make_async_remote_copy(
            src_ref=SB2.at[d, at : at + size], dst_ref=R2.at[src, at : at + size],
            send_sem=send2.at[part, d], recv_sem=recv2.at[part, src], device_id={"az": d},
        )

    def returned(part):
        at, size = BACKS[part]
        for k in range(1, 8):
            back(part, lax.rem(az + k, n_az), az).start()
        R2[az, at : at + size] = SB2[az, at : at + size]

    arrived(0)
    neighbours()
    edges(0)
    filtered(0)
    returned(0)
    for l in range(LT):
        for s in range(2):

            @pl.when(gx == (up_relay if s == 0 else down_relay)[l])
            def _():
                leg(l, s).wait_recv()
                relay(l, s).start()

    lax.fori_loop(N1, 17, outer, 0)
    arrived(1)
    edges(1)
    filtered(1)
    returned(1)

    for s in range(2):
        for l in range(LT):
            swirls[l][s].wait_recv()

    def pads(p, _):
        for l in range(LT):
            for r0 in (0, 40):
                r = pl.ds(r0, 8)
                st = [ST[l, f, p, r] for f in range(5)]
                u, v, w, a, b, c, pressure, h = prims(st)
                FX[l, 2, p, r] = st[3] * u
                swirl_fluxes(l, p, r, st[2], st[3], w, c, pressure, h)
        return 0

    lax.fori_loop(1, 17, pads, 0)

    def finish(p, _):
        step = (0.5 * time_step) * inv_dx[p - 1]
        for l in range(LT):
            for f in range(5):
                for g in range(4):
                    r = pl.ds(8 + 8 * g, 8)
                    if f == 0:
                        above, below = ST[l, 1, p + 1, r], ST[l, 1, p - 1, r]
                    else:
                        above, below = FX[l, f - 1, p + 1, r], FX[l, f - 1, p - 1, r]
                    c = SWIRL[f]
                    turn = FX[l, c, p, pl.ds(9 + 8 * g, 8)] - FX[l, c, p, pl.ds(7 + 8 * g, 8)]
                    x = PART[l, f, p - 1, pl.ds(8 * g, 8)]
                    x = x - step * (above - below) - LC[2, l] * turn
                    out[f, p - 1, 8 * g : 8 * g + 8, l * 128 : (l + 1) * 128] = x
        return 0

    lax.fori_loop(2, 16, finish, 0)
    for s in range(2):
        p = 0 if s == 0 else 17

        @pl.when(gets_from[s])
        def _():
            for l in range(LT):
                axials[l][s].wait_recv()
                for g in range(4):
                    r = pl.ds(8 + 8 * g, 8)
                    axial_fluxes(l, p, r, [ST[l, f, p, r] for f in range(5)])

        @pl.when(jnp.logical_not(gets_from[s]))
        def _():
            for l in range(LT):
                for g in range(4):
                    r = pl.ds(8 + 8 * g, 8)
                    ST[l, 1, p, r] = zero
                    for k in range(4):
                        FX[l, k, p, r] = zero

        finish(1 if s == 0 else 16, 0)

    for s in range(2):
        for l in range(LT):
            swirls[l][s].wait_send()

        @pl.when(sends_to[s])
        def _():
            for l in range(LT):
                axials[l][s].wait_send()
            for y in range(2):
                hello(s, y).wait_send()

        for l in range(LT):

            @pl.when(gx == (up_relay if s == 0 else down_relay)[l])
            def _():
                relay(l, s).wait_send()

    for k in range(1, 8):
        e = lax.rem(az + k, n_az)
        for part in range(2):
            forth(part, e).wait_send()
            back(part, e, az).wait_send()
            back(part, e, e).wait_recv()


def write(partial, filtered, out, T0, sem, sem0):
    rest = pltpu.make_async_copy(
        partial.at[:, :, :, 128:NR], out.at[:, :, :, 128:NR], sem
    )
    rest.start()
    lane = lax.broadcasted_iota(jnp.int32, (8, 128), 1)

    def tile(q):
        return pltpu.make_async_copy(
            T0.at[:, pl.ds(4 * q, 4)], out.at[:, pl.ds(4 * q, 4), :, 0:128], sem0.at[q]
        )

    def merge(q, _):
        for i in range(4):
            p = 4 * q + i
            for f in range(5):
                for g in range(4):
                    if f != 2:
                        e = q if f < 2 else q + 4
                        s = f if f < 2 else f - 3
                        x = filtered[e, 32 * s + 8 * g : 32 * s + 8 * g + 8]
                        base = 32 * i
                    else:
                        e = q if i < 2 else q + 4
                        x = filtered[e, 64 + 8 * (g % 2) : 72 + 8 * (g % 2)]
                        base = 32 * (i % 2) + 64 * (g // 2)
                    if base:
                        x = pltpu.roll(x, 128 - base, 1)
                    old = partial[f, p, 8 * g : 8 * g + 8, 0:128]
                    T0[f, p, 8 * g : 8 * g + 8] = jnp.where(lane < CYCLE, x, old)
        tile(q).start()
        return 0

    lax.fori_loop(0, 4, merge, 0)
    for q in range(4):
        tile(q).wait()
    rest.wait()


def solution(mesh):
    fwd, inv = tables()

    def body(state, sponge_level, inv_dx, inv_dr, target, cutoff):
        f32 = jnp.float32
        hbm = pl.BlockSpec(memory_space=pltpu.HBM)
        vmem = pl.BlockSpec(memory_space=pltpu.VMEM)
        dma = pltpu.SemaphoreType.DMA
        args = (state, sponge_level, inv_dr.reshape(1, NR), target, jnp.asarray(fwd), jnp.asarray(inv), inv_dx, cutoff)
        args = [pltpu.with_memory_space_constraint(x, pltpu.HBM) for x in args]
        partial, filtered = pl.pallas_call(
            kernel,
            out_shape=(pltpu.VMEM(state.shape, f32), pltpu.VMEM((8, BACK, 128), f32)),
            in_specs=[hbm] * 8,
            out_specs=(vmem, vmem),
            scratch_shapes=[
                pltpu.VMEM((LT, 5, 18, 48, 128), f32),
                pltpu.VMEM((LT, 8, 18, 48, 128), f32),
                pltpu.VMEM((LT, 5, 16, 32, 128), f32),
                pltpu.VMEM((LT, 16, 32, 128), jnp.int32),
                pltpu.VMEM((5, NR), f32),
                pltpu.VMEM((1, NR), f32),
                pltpu.VMEM(fwd.shape, jnp.bfloat16),
                pltpu.VMEM(inv.shape, jnp.bfloat16),
                pltpu.VMEM((9, LT, 8, 128), f32),
                pltpu.VMEM((13, 8, 128), f32),
                pltpu.VMEM((4, 5, 32, 128), f32),
                pltpu.VMEM((6, 5, 32, 128), f32),
                pltpu.VMEM((4, 5, 48, 128), f32),
                pltpu.VMEM((8, ROWS, 128), f32),
                pltpu.VMEM((8, ROWS, 128), f32),
                pltpu.VMEM((8, BACK, 128), f32),
                pltpu.VMEM((2, 2, 24, 128), f32),
                pltpu.VMEM((8, 24, 128), f32),
                pltpu.VMEM((5, 1, CELLS, 128), f32),
                pltpu.VMEM((80, 128), f32),
                pltpu.SMEM((PL_DEV,), f32),
                pltpu.SMEM((CYCLE,), jnp.int32),
                dma((2 * LT,)),
                dma((6,)),
                dma((LT, 2)),
                dma((LT, 2)),
                dma((LT, 2)),
                dma((LT, 2)),
                dma((2, 8)),
                dma((2, 8)),
                dma((2, 8)),
                dma((2, 8)),
                dma((2, 2)),
                dma((8,)),
                dma(()),
                dma(()),
            ],
            compiler_params=pltpu.CompilerParams(collective_id=0, has_side_effects=True, vmem_limit_bytes=48 << 20),
        )(*args)
        partial, filtered = (pltpu.with_memory_space_constraint(x, pltpu.VMEM) for x in (partial, filtered))
        return pl.pallas_call(
            write,
            out_shape=jax.ShapeDtypeStruct(state.shape, f32),
            in_specs=[vmem, vmem],
            out_specs=hbm,
            scratch_shapes=[pltpu.VMEM((5, PL_DEV, CELLS, 128), f32), dma(()), dma((4,))],
            compiler_params=pltpu.CompilerParams(vmem_limit_bytes=4 << 20),
        )(partial, filtered)

    return jax.shard_map(
        body,
        mesh=mesh,
        in_specs=(P(None, "gx", "az", None), P("gx", "az", None), P("gx"), P(), P(), P()),
        out_specs=P(None, "gx", "az", None),
        check_vma=False,
    )
```

time: 45 us -> 26.9 us (0.60)
  the two profiles are of different devices: /device:TPU:26 before, /device:TPU:30 now
where the time goes in v2:
time: 26.9 us; the launch traced here: 26.8 us
  Pallas kernels  26.8 us (100%)
    pallas_call x1, Pallas kernels, body(): pl.pallas_call(kernel, out_shape=(pltpu.VMEM(state.shape, f32), pltpu.VME...  24.4 us
    pallas_call x1, Pallas kernels, body(): pl.pallas_call(write, out_shape=jax.ShapeDtypeStruct(state.shape, f32), i...  2.37 us

profile of v2, /device:TPU:30, one launch (start us, length us, event | category | flops | bytes accessed | tf_op | source)
XLA Modules:
  0.0 26.8 jit_solution(8137583137928922005)
XLA Ops:
  0.0 24.4 %shard_map.82 = (f32[5,16,32,512]{3,2,1,0:T(8,128)S(1)}, f32[8,80,128]{2,1,0:T(8,128)S(1)}) custom-call(f32[5,16,32,512]{3,2,1,0:T(8,128)} %state.1, s32[16,32,512]{2,1,0:T(8,128)} %sponge.1, f32[1,512]{1,0:T(1,128)} %bitcast.1, f32[5,512]{1,0:T(8,128)} %target.1, bf16[160,256]{1,0:T(8,128)(2,1)} %constant.4.clone.fwd_t, ...), custom_call_target="tpu_custom_call" | custom-call | tf_op jit(solution)/shard_map/pallas_call | solution.py:695
  24.4 2.4 %shard_map.83 = f32[5,16,32,512]{3,2,1,0:T(8,128)} custom-call(f32[5,16,32,512]{3,2,1,0:T(8,128)S(1)} %get-tuple-element.7.partial, f32[8,80,128]{2,1,0:T(8,128)S(1)} %get-tuple-element.8.filtered), custom_call_target="tpu_custom_call" | custom-call | tf_op jit(solution)/shard_map/pallas_call | solution.py:741

commit v3 on v2

--- a/solution.py
+++ b/solution.py
@@ -19,7 +19,9 @@
 
 ROWS = 88
 BACK = 80
-N1 = 12
+N1 = 14
+ORDER = (1, 2, 3, 4, 5, 6, 7)
+SPREAD = (1, 1, 1, 1)
 
 
 def tables():
@@ -64,7 +66,7 @@
     east, west = lax.rem(az + 1, n_az), lax.rem(az + n_az - 1, n_az)
     partner = lax.rem(az + 4, n_az)
     mid = n_gx // 2
-    up_relay = [mid - 1 - 2 * l for l in range(LT)]
+    up_relay = [1 + 2 * l for l in range(LT)]
     down_relay = [n_gx - 1 - 2 * l for l in range(LT)]
     first_x, last_x = lax.rem(az, 4) == 0, lax.rem(az, 4) == 3
 
@@ -259,6 +261,12 @@
                 PI[q, f, o] = part
         return 0
 
+    def send_swirl(when):
+        for l in range(LT):
+            if SPREAD[l] == when:
+                for s in range(2):
+                    swirls[l][s].start()
+
     lax.fori_loop(0, 4, inner, 0)
 
     def hello(side, y):
@@ -283,6 +291,22 @@
             else:
                 s = f if f < 2 else f - 3
                 HS[side, f // 3, 8 * s : 8 * s + 8] = got
+
+    def leg(l, side):
+        plane = 15 if side == 0 else 0
+        return pltpu.make_async_remote_copy(
+            src_ref=state.at[:, plane : plane + 1, :, lanes(l)], dst_ref=RL,
+            send_sem=ax_send.at[l, side], recv_sem=rl_recv,
+            device_id={"gx": jnp.int32((up_relay if side == 0 else down_relay)[l]), "az": partner},
+        )
+
+    def relay(l, side):
+        slot = 0 if side == 0 else 17
+        return pltpu.make_async_remote_copy(
+            src_ref=RL, dst_ref=ST.at[l, :, slot : slot + 1, 8:40, :],
+            send_sem=rl_send, recv_sem=ax_recv.at[l, side],
+            device_id={"gx": jnp.int32(mid if side == 0 else mid - 1), "az": partner},
+        )
 
     PARTS = ((0, 40), (40, 48))
 
@@ -338,13 +362,12 @@
 
     def sent(part):
         at, size = PARTS[part]
-        for k in range(1, 8):
+        for k in ORDER:
             forth(part, lax.rem(az + k, n_az)).start()
         RB[az, at : at + size] = SB[az, at : at + size]
 
     lax.fori_loop(0, 4, group_a, 0)
     pl.semaphore_wait(barrier, greeted)
-    sent(0)
     for side in range(2):
 
         @pl.when(sends_to[side])
@@ -352,41 +375,23 @@
             for y in range(2):
                 hello(side, y).start()
 
+    for s in range(2):
+
+        @pl.when(gx == (mid - 1, mid)[s])
+        def _():
+            for l in range(LT):
+                leg(l, s).start()
+
+    sent(0)
     lax.fori_loop(0, 4, group_b, 0)
     sent(1)
-    for l in range(LT):
-        for s in range(2):
-            swirls[l][s].start()
+    send_swirl(1)
     for s in range(2):
 
         @pl.when(direct[s])
         def _():
             for l in range(LT):
                 axials[l][s].start()
-
-    def leg(l, side):
-        plane = 15 if side == 0 else 0
-        return pltpu.make_async_remote_copy(
-            src_ref=state.at[:, plane : plane + 1, :, lanes(l)], dst_ref=RL,
-            send_sem=ax_send.at[l, side], recv_sem=rl_recv,
-            device_id={"gx": jnp.int32((up_relay if side == 0 else down_relay)[l]), "az": partner},
-        )
-
-    def relay(l, side):
-        slot = 0 if side == 0 else 17
-        return pltpu.make_async_remote_copy(
-            src_ref=RL, dst_ref=ST.at[l, :, slot : slot + 1, 8:40, :],
-            send_sem=rl_send, recv_sem=ax_recv.at[l, side],
-            device_id={"gx": jnp.int32(mid if side == 0 else mid - 1), "az": partner},
-        )
-
-    starts = (gx == mid - 1, gx == mid)
-    for s in range(2):
-
-        @pl.when(starts[s])
-        def _():
-            for l in range(LT):
-                leg(l, s).start()
 
     SWIRL = (7, 2, 4, 5, 6)
 
@@ -539,7 +544,7 @@
 
     def returned(part):
         at, size = BACKS[part]
-        for k in range(1, 8):
+        for k in ORDER:
             back(part, lax.rem(az + k, n_az), az).start()
         R2[az, at : at + size] = SB2[az, at : at + size]
 
@@ -548,54 +553,53 @@
     edges(0)
     filtered(0)
     returned(0)
-    for l in range(LT):
-        for s in range(2):
-
-            @pl.when(gx == (up_relay if s == 0 else down_relay)[l])
-            def _():
-                leg(l, s).wait_recv()
-                relay(l, s).start()
-
+    send_swirl(2)
     lax.fori_loop(N1, 17, outer, 0)
     arrived(1)
     edges(1)
     filtered(1)
     returned(1)
-
-    for s in range(2):
-        for l in range(LT):
+    for l in range(LT):
+        for s in range(2):
+
+            @pl.when(gx == (up_relay if s == 0 else down_relay)[l])
+            def _():
+                leg(l, s).wait_recv()
+                relay(l, s).start()
+
+
+    def finish(l, p):
+        step = (0.5 * time_step) * inv_dx[p - 1]
+        for r0 in (0, 40):
+            r = pl.ds(r0, 8)
+            st = [ST[l, f, p, r] for f in range(5)]
+            u, v, w, a, b, c, pressure, h = prims(st)
+            FX[l, 2, p, r] = st[3] * u
+            swirl_fluxes(l, p, r, st[2], st[3], w, c, pressure, h)
+        for f in range(5):
+            for g in range(4):
+                r = pl.ds(8 + 8 * g, 8)
+                if f == 0:
+                    above, below = ST[l, 1, p + 1, r], ST[l, 1, p - 1, r]
+                else:
+                    above, below = FX[l, f - 1, p + 1, r], FX[l, f - 1, p - 1, r]
+                c = SWIRL[f]
+                turn = FX[l, c, p, pl.ds(9 + 8 * g, 8)] - FX[l, c, p, pl.ds(7 + 8 * g, 8)]
+                x = PART[l, f, p - 1, pl.ds(8 * g, 8)]
+                x = x - step * (above - below) - LC[2, l] * turn
+                out[f, p - 1, 8 * g : 8 * g + 8, l * 128 : (l + 1) * 128] = x
+
+    for l in range(LT):
+        for s in range(2):
             swirls[l][s].wait_recv()
 
-    def pads(p, _):
-        for l in range(LT):
-            for r0 in (0, 40):
-                r = pl.ds(r0, 8)
-                st = [ST[l, f, p, r] for f in range(5)]
-                u, v, w, a, b, c, pressure, h = prims(st)
-                FX[l, 2, p, r] = st[3] * u
-                swirl_fluxes(l, p, r, st[2], st[3], w, c, pressure, h)
-        return 0
-
-    lax.fori_loop(1, 17, pads, 0)
-
-    def finish(p, _):
-        step = (0.5 * time_step) * inv_dx[p - 1]
-        for l in range(LT):
-            for f in range(5):
-                for g in range(4):
-                    r = pl.ds(8 + 8 * g, 8)
-                    if f == 0:
-                        above, below = ST[l, 1, p + 1, r], ST[l, 1, p - 1, r]
-                    else:
-                        above, below = FX[l, f - 1, p + 1, r], FX[l, f - 1, p - 1, r]
-                    c = SWIRL[f]
-                    turn = FX[l, c, p, pl.ds(9 + 8 * g, 8)] - FX[l, c, p, pl.ds(7 + 8 * g, 8)]
-                    x = PART[l, f, p - 1, pl.ds(8 * g, 8)]
-                    x = x - step * (above - below) - LC[2, l] * turn
-                    out[f, p - 1, 8 * g : 8 * g + 8, l * 128 : (l + 1) * 128] = x
-        return 0
-
-    lax.fori_loop(2, 16, finish, 0)
+        def planes(i, _, l=l):
+            for k in range(2):
+                finish(l, 2 * i + k)
+            return 0
+
+        lax.fori_loop(1, 8, planes, 0)
+
     for s in range(2):
         p = 0 if s == 0 else 17
 
@@ -616,7 +620,8 @@
                     for k in range(4):
                         FX[l, k, p, r] = zero
 
-        finish(1 if s == 0 else 16, 0)
+        for l in range(LT):
+            finish(l, 1 if s == 0 else 16)
 
     for s in range(2):
         for l in range(LT):
@@ -644,10 +649,14 @@
 
 
 def write(partial, filtered, out, T0, sem, sem0):
-    rest = pltpu.make_async_copy(
-        partial.at[:, :, :, 128:NR], out.at[:, :, :, 128:NR], sem
-    )
-    rest.start()
+    rests = [
+        pltpu.make_async_copy(
+            partial.at[f, :, :, 128:NR], out.at[f, :, :, 128:NR], sem.at[f]
+        )
+        for f in range(5)
+    ]
+    for rest in rests:
+        rest.start()
     lane = lax.broadcasted_iota(jnp.int32, (8, 128), 1)
 
     def tile(q):
@@ -679,7 +688,8 @@
     lax.fori_loop(0, 4, merge, 0)
     for q in range(4):
         tile(q).wait()
-    rest.wait()
+    for rest in rests:
+        rest.wait()
 
 
 def solution(mesh):
@@ -743,7 +753,7 @@
             out_shape=jax.ShapeDtypeStruct(state.shape, f32),
             in_specs=[vmem, vmem],
             out_specs=hbm,
-            scratch_shapes=[pltpu.VMEM((5, PL_DEV, CELLS, 128), f32), dma(()), dma((4,))],
+            scratch_shapes=[pltpu.VMEM((5, PL_DEV, CELLS, 128), f32), dma((5,)), dma((4,))],
             compiler_params=pltpu.CompilerParams(vmem_limit_bytes=4 << 20),
         )(partial, filtered)
 

time: 26.9 us -> 24.5 us (0.911)
  the two profiles are of different devices: /device:TPU:30 before, /device:TPU:1 now
where the time goes in v3:
time: 24.5 us; the launch traced here: 24.2 us
  Pallas kernels  24.2 us (99%)
    pallas_call x1, Pallas kernels, body(): pl.pallas_call(kernel, out_shape=(pltpu.VMEM(state.shape, f32), pltpu.VME...  21.7 us
    pallas_call x1, Pallas kernels, body(): pl.pallas_call(write, out_shape=jax.ShapeDtypeStruct(state.shape, f32), i...  2.41 us

profile of v3, /device:TPU:1, one launch (start us, length us, event | category | flops | bytes accessed | tf_op | source)
XLA Modules:
  0.0 24.2 jit_solution(3684770335576617523)
XLA Ops:
  0.0 21.7 %shard_map.82 = (f32[5,16,32,512]{3,2,1,0:T(8,128)S(1)}, f32[8,80,128]{2,1,0:T(8,128)S(1)}) custom-call(f32[5,16,32,512]{3,2,1,0:T(8,128)} %state.1, s32[16,32,512]{2,1,0:T(8,128)} %sponge.1, f32[1,512]{1,0:T(1,128)} %bitcast.1, f32[5,512]{1,0:T(8,128)} %target.1, bf16[160,256]{1,0:T(8,128)(2,1)} %constant.4.clone.fwd_t, ...), custom_call_target="tpu_custom_call" | custom-call | tf_op jit(solution)/shard_map/pallas_call | solution.py:705
  21.7 2.4 %shard_map.83 = f32[5,16,32,512]{3,2,1,0:T(8,128)} custom-call(f32[5,16,32,512]{3,2,1,0:T(8,128)S(1)} %get-tuple-element.7.partial, f32[8,80,128]{2,1,0:T(8,128)S(1)} %get-tuple-element.8.filtered), custom_call_target="tpu_custom_call" | custom-call | tf_op jit(solution)/shard_map/pallas_call | solution.py:751
